TPU v7x, 32 devices: a whole 2x2x4 slice. The times are simulated.
32 devices in a mesh: rows: 8 (over z, y), cls: 4 (over x, core).
Axes of the slice: x: 2, y: 2, z: 4, core: 2. Of those that a mesh axis runs over, the one named last changes fastest.
Arguments:
- features: bfloat16 [6144, 2048], P('rows', 'cls'), may hold values from -32 to 32
- prototypes: bfloat16 [2048, 16384], P('rows', 'cls'), may hold values from -1 to 1
Outputs:
- grad_proto: float32 [2048, 16384], P('rows', 'cls')
All inputs are finite; a program needn't handle non-finite values.
Results may differ from a plain program's by a relative error of at most 0.02.
Values may be sent and summed in bfloat16 or wider, within the bound.
A program may use at most 128 MiB of HBM per device.

v0:
```python
import jax
import jax.numpy as jnp
from jax import lax
from jax.sharding import PartitionSpec as P

ITERS = 3
code_temp = 0.2
loss_temp = 0.3


def local(features, prototypes):
    gathered = lax.all_gather(features, "cls", axis=1, tiled=True)
    local_rows = gathered.shape[0]
    local_classes = prototypes.shape[1]
    balance_ratio = float(local_rows * lax.axis_size("rows")) / float(
        local_classes * lax.axis_size("cls")
    )
    columns = gathered
    scores = jnp.dot(
        columns,
        lax.all_gather(prototypes, "rows", axis=0, tiled=True),
        preferred_element_type=jnp.float32,
    )
    local_top = jnp.max(scores, axis=1)
    row_top = lax.pmax(local_top, "cls")
    shifted = scores - row_top[:, None]
    exp_codes = jnp.exp(shifted / code_temp)
    exp_loss = jnp.exp(shifted / loss_temp)
    sink_total, soft_total = lax.psum(
        (jnp.sum(exp_codes, axis=1), jnp.sum(exp_loss, axis=1)), "cls"
    )
    codes = exp_codes / sink_total[:, None]
    for sweep in range(ITERS):
        col_mass = lax.psum(jnp.sum(codes, axis=0), "rows")
        codes = codes * (balance_ratio / col_mass)[None, :]
        row_mass = lax.psum(jnp.sum(codes, axis=1), "cls")
        codes = codes / row_mass[:, None]
    probs_loss = exp_loss / soft_total[:, None]
    slope = ((probs_loss - codes) / loss_temp).astype(jnp.bfloat16)
    columns = gathered
    return lax.psum_scatter(
        lax.dot_general(
            columns, slope, (((0,), (0,)), ((), ())), preferred_element_type=jnp.float32
        ).astype(jnp.bfloat16),
        "rows",
        scatter_dimension=0,
        tiled=True,
    ).astype(jnp.float32)


def solution(mesh):
    return jax.shard_map(
        local,
        mesh=mesh,
        in_specs=(P("rows", "cls"), P("rows", "cls")),
        out_specs=P("rows", "cls"),
        check_vma=False,
    )
```

profile of v0, /device:TPU:0, one launch (start us, length us, event | category | flops | bytes accessed | tf_op | source)
XLA Modules:
  0.0 786.4 jit_solution(6704144554605490783)
XLA Ops:
  6.5 0.7 all-gather.3.cloned.1.call-update
  7.3 0.7 all-gather.5.cloned.1.call-update
  8.0 0.0 reduce-scatter.2.cloned.1.call-start
  8.1 32.1 %all-gather.3.cloned.1.call-done = bf16[768,2048]{1,0:T(8,128)(2,1)} async-done(((bf16[768,512]{1,0:T(8,128)(2,1)}), bf16[768,2048]{1,0:T(8,128)(2,1)}) %all-gather.3.cloned.1.call-update) | async-done | bytes 3145744 | tf_op jit(solution)/shard_map/all_gather | solution.py:12
  40.2 229.8 %all-gather.5.cloned.1.call-done = bf16[2048,4096]{1,0:T(8,128)(2,1)} async-done(((bf16[256,4096]{1,0:T(8,128)(2,1)}), bf16[2048,4096]{1,0:T(8,128)(2,1)}) %all-gather.5.cloned.1.call-update) | async-done | bytes 16777232 | tf_op jit(solution)/shard_map/all_gather | solution.py:21
  270.0 20.3 %fusion.8 = (f32[768]{0:T(1024)S(1)}, f32[768,4096]{1,0:T(8,128)}) fusion(bf16[768,2048]{1,0:T(8,128)(2,1)} %all-gather.3.cloned.1.call-done, bf16[2048,4096]{1,0:T(8,128)(2,1)} %all-gather.5.cloned.1.call-done), kind=kOutput, calls=%fused_computation.19 | convolution fusion | flops 12888046592 | bytes 32508928 | tf_op jit(solution)/shard_map/dot_general | solution.py:19
  290.3 6.1 pmax.7
  296.4 7.1 fusion
  303.5 6.1 psum.57
  309.7 11.3 %fusion.6 = (f32[4096]{0:T(1024)S(1)}, f32[768,4096]{1,0:T(8,128)}) fusion(f32[768]{0:T(1024)S(1)} %psum.57, f32[768,4096]{1,0:T(8,128)} %get-tuple-element.14, f32[768]{0:T(1024)S(1)} %pmax.7), kind=kLoop, calls=%fused_computation.18 | loop fusion | flops 12578816 | bytes 25188352 | tf_op jit(solution)/shard_map/reduce_sum | solution.py:34
  320.9 34.6 %psum.58 = f32[4096]{0:T(1024)S(1)} all-reduce(f32[4096]{0:T(1024)S(1)} %get-tuple-element.11), channel_id=1, replica_groups=mesh['rows'=8,'cls'=4] {'rows'}, use_global_device_ids=true, to_apply=%region_7.0 | all-reduce | flops 4096 | bytes 32768 | tf_op jit(solution)/shard_map/psum | solution.py:34
  355.6 5.5 multiply_reduce_fusion.2
  361.1 5.8 psum.59
  366.8 6.4 fusion.4
  373.3 33.2 %psum.60 = f32[4096]{0:T(1024)S(1)} all-reduce(f32[4096]{0:T(1024)S(1)} %fusion.4), channel_id=1, replica_groups=mesh['rows'=8,'cls'=4] {'rows'}, use_global_device_ids=true, to_apply=%region_11.0 | all-reduce | flops 4096 | bytes 32768 | tf_op jit(solution)/shard_map/psum | solution.py:34
  406.5 6.0 multiply_reduce_fusion.1
  412.4 5.8 psum.61
  418.2 11.3 %fusion.5 = (f32[4096]{0:T(1024)S(1)}, f32[768,4096]{1,0:T(8,128)}) fusion(f32[768]{0:T(1024)S(1)} %psum.61, f32[4096]{0:T(1024)S(1)} %broadcast_divide_fusion.1, f32[768]{0:T(1024)S(1)} %psum.59, f32[768,4096]{1,0:T(8,128)} %get-tuple-element.12, f32[4096]{0:T(1024)S(1)} %broadcast_divide_fusion.2), kind=kLoop, calls=%fused_computation.17 | loop fusion | flops 15724544 | bytes 25221120 | tf_op jit(solution)/shard_map/reduce_sum | solution.py:34
  429.5 33.2 %psum.62 = f32[4096]{0:T(1024)S(1)} all-reduce(f32[4096]{0:T(1024)S(1)} %get-tuple-element.9), channel_id=1, replica_groups=mesh['rows'=8,'cls'=4] {'rows'}, use_global_device_ids=true, to_apply=%region_15.0 | all-reduce | flops 4096 | bytes 32768 | tf_op jit(solution)/shard_map/psum | solution.py:34
  462.7 5.5 multiply_reduce_fusion
  468.2 5.9 all-reduce
  474.1 22.6 %convert_bitcast_fusion = bf16[2048,4096]{0,1:T(8,128)(2,1)} fusion(bf16[768,2048]{1,0:T(8,128)(2,1)S(1)} %copy-done, f32[768,4096]{1,0:T(8,128)} %get-tuple-element.10, f32[768,4096]{1,0:T(8,128)} %get-tuple-element.14, f32[768]{0:T(1024)S(1)} %get-tuple-element.7, f32[4096]{0:T(1024)S(1)} %broadcast_divide_fusion, f32[768]{0:T(1024)S(1)} %get-tuple-element.8, ...), kind=kOutput, calls=%fused_computation | convolution fusion | flops 12918456320 | bytes 45114368 | tf_op jit(solution)/shard_map/dot_general | solution.py:42
  496.8 278.8 %reduce-scatter.2.cloned.1.call-done = bf16[256,4096]{0,1:T(8,128)(2,1)} async-done(((bf16[2048,4096]{0,1:T(8,128)(2,1)}), bf16[256,4096]{0,1:T(8,128)(2,1)}) %reduce-scatter.2.cloned.1.call-update) | async-done | bytes 2097168 | tf_op jit(solution)/shard_map/reduce_scatter | solution.py:41
  775.6 4.3 copy.3
  (8 shorter events, 0.1 us)
Async XLA Ops:
  6.5 33.6 %all-gather.3.cloned.1.call-start = ((), (), s32[]{:S(2)}) async-start(), calls=%async_computation.1 | async-start | bytes 3932160 | tf_op jit(solution)/shard_map/all_gather | solution.py:12
  7.3 262.7 %all-gather.5.cloned.1.call-start = ((), (), s32[]{:S(2)}) async-start(), calls=%async_computation.2 | async-start | bytes 18874368 | tf_op jit(solution)/shard_map/all_gather | solution.py:21
  8.0 767.6 %reduce-scatter.2.cloned.1.call-start = ((), (), s32[]{:S(2)}) async-start(), calls=%async_computation.3 | async-start | bytes 18874368 | tf_op jit(solution)/shard_map/reduce_scatter | solution.py:41
  429.5 44.6 %copy-start = (bf16[768,2048]{1,0:T(8,128)(2,1)S(1)}, bf16[768,2048]{1,0:T(8,128)(2,1)}, u32[]{:S(2)}) copy-start(bf16[768,2048]{1,0:T(8,128)(2,1)} %all-gather.3.cloned.1.call-done) | copy-start | bytes 9437188
Sparse Core Ops, SparseCore 0:
  8.9 31.2 all-gather.2
  42.3 227.6 all-gather.4
  496.9 278.6 reduce-scatter.1
where the time goes:
time: 787 us; the launch traced here: 786 us
  waiting for transfers between devices  542 us (69%)
  blocking collectives  131 us (17%)
  other arithmetic  53.1 us (7%)
  matrix products  42.9 us (5%)
  between operations  13.1 us (2%)
    reduce_scatter x1, waiting for transfers between devices, local(): lax.psum_scatter(lax.dot_general(columns, slope, (((0,), (0,)), ((), ()))...  279 us
    all_gather x1, waiting for transfers between devices, local(): lax.all_gather(prototypes, 'rows', axis=0, tiled=True)  230 us
    psum x3, blocking collectives, local(): col_mass = lax.psum(jnp.sum(codes, axis=0), 'rows')  101 us
    all_gather x1, waiting for transfers between devices, local(): gathered = lax.all_gather(features, 'cls', axis=1, tiled=True)  32.1 us
    reduce_sum x3, other arithmetic, local(): col_mass = lax.psum(jnp.sum(codes, axis=0), 'rows')  29 us
    dot_general x1, matrix products, local(): lax.dot_general(columns, slope, (((0,), (0,)), ((), ())), preferred_eleme...  22.6 us
    dot_general x1, matrix products, local(): jnp.dot(columns, lax.all_gather(prototypes, 'rows', axis=0, tiled=True),...  20.3 us
    psum x3, blocking collectives, local(): row_mass = lax.psum(jnp.sum(codes, axis=1), 'cls')  17.4 us
  transfers between devices with their start and end apart: 3, of which 3 were waited for; matrix products, arithmetic and copies ran while one was open for 0% of the time, Pallas kernels for 0%

commit v1 on v0

--- a/solution.py
+++ b/solution.py
@@ -9,7 +9,12 @@
 
 
 def local(features, prototypes):
-    gathered = lax.all_gather(features, "cls", axis=1, tiled=True)
+    ring = [features]
+    for hop in range(3):
+        ring.append(lax.ppermute(ring[-1], "cls", [(dev, (dev + 1) % 4) for dev in range(4)]))
+    gathered = jnp.roll(
+        jnp.concatenate(ring[::-1], axis=1), (lax.axis_index("cls") + 1) * ring[0].shape[1], axis=1
+    )
     local_rows = gathered.shape[0]
     local_classes = prototypes.shape[1]
     balance_ratio = float(local_rows * lax.axis_size("rows")) / float(

time: 787 us -> 758 us (0.963)
  waiting for transfers between devices: 542 us -> 502 us
    all_gather x1, waiting for transfers between devices: 230 us -> 188 us  [local(): lax.all_gather(prototypes, 'rows', axis=0, tiled=True)]
    ppermute x0 -> x3, waiting for transfers between devices: none -> 34.6 us  [local(): lax.ppermute(ring[-1], 'cls', [(dev, (dev + 1) % 4) for dev in range(4)])]
    all_gather x1 -> x0, waiting for transfers between devices: 32.1 us -> none  [local(): gathered = lax.all_gather(features, 'cls', axis=1, tiled=True)]
    unnamed x2 -> x9, local copies, waits for them, and re-layouts: 0.01 us -> 8.16 us
  transfers between devices with their start and end apart: 3 -> 5, of which waited for: 3 -> 5; matrix products, arithmetic and copies ran while one was open for 0% -> 1% of each run, Pallas kernels for 0% -> 0%
where the time goes in v1:
time: 758 us; the launch traced here: 757 us
  waiting for transfers between devices  502 us (66%)
  blocking collectives  130 us (17%)
  other arithmetic  57.2 us (8%)
  matrix products  44.7 us (6%)
  between operations  13.4 us (2%)
  local copies, waits for them, and re-layouts  9.14 us (1%)
    reduce_scatter x1, waiting for transfers between devices, local(): lax.psum_scatter(lax.dot_general(columns, slope, (((0,), (0,)), ((), ()))...  278 us
    all_gather x1, waiting for transfers between devices, local(): lax.all_gather(prototypes, 'rows', axis=0, tiled=True)  188 us
    psum x3, blocking collectives, local(): col_mass = lax.psum(jnp.sum(codes, axis=0), 'rows')  101 us
    ppermute x3, waiting for transfers between devices, local(): lax.ppermute(ring[-1], 'cls', [(dev, (dev + 1) % 4) for dev in range(4)])  34.6 us
    reduce_sum x3, other arithmetic, local(): col_mass = lax.psum(jnp.sum(codes, axis=0), 'rows')  29 us
    dot_general x1, matrix products, local(): lax.dot_general(columns, slope, (((0,), (0,)), ((), ())), preferred_eleme...  24.4 us
    dot_general x1, matrix products, local(): jnp.dot(columns, lax.all_gather(prototypes, 'rows', axis=0, tiled=True),...  20.3 us
    psum x3, blocking collectives, local(): row_mass = lax.psum(jnp.sum(codes, axis=1), 'cls')  17.4 us
  transfers between devices with their start and end apart: 5, of which 5 were waited for; matrix products, arithmetic and copies ran while one was open for 1% of the time, Pallas kernels for 0%

profile of v1, /device:TPU:0, one launch (start us, length us, event | category | flops | bytes accessed | tf_op | source)
XLA Modules:
  0.0 757.0 jit_solution(1527703889865508203)
XLA Ops:
  7.8 11.8 %collective-permute-done = bf16[768,512]{1,0:T(8,128)(2,1)S(1)} collective-permute-done((bf16[768,512]{1,0:T(8,128)(2,1)}, bf16[768,512]{1,0:T(8,128)(2,1)S(1)}, u32[]{:S(2)}, u32[]{:S(2)}) %collective-permute-start) | collective-permute-done | bytes 786464 | tf_op jit(solution)/shard_map/ppermute | solution.py:14
  19.7 11.4 %collective-permute-done.1 = bf16[768,512]{1,0:T(8,128)(2,1)S(1)} collective-permute-done((bf16[768,512]{1,0:T(8,128)(2,1)S(1)}, bf16[768,512]{1,0:T(8,128)(2,1)S(1)}, u32[]{:S(2)}, u32[]{:S(2)}) %collective-permute-start.1) | collective-permute-done | bytes 786464 | tf_op jit(solution)/shard_map/ppermute | solution.py:14
  31.0 11.4 %collective-permute-done.2 = bf16[768,512]{1,0:T(8,128)(2,1)S(1)} collective-permute-done((bf16[768,512]{1,0:T(8,128)(2,1)S(1)}, bf16[768,512]{1,0:T(8,128)(2,1)S(1)}, u32[]{:S(2)}, u32[]{:S(2)}) %collective-permute-start.2) | collective-permute-done | bytes 786464 | tf_op jit(solution)/shard_map/ppermute | solution.py:14
  45.4 2.1 constant_dynamic-update-slice_fusion.4
  51.6 188.2 %all-gather.2.cloned.1.call-done = bf16[2048,4096]{1,0:T(8,128)(2,1)} async-done(((bf16[256,4096]{1,0:T(8,128)(2,1)}), bf16[2048,4096]{1,0:T(8,128)(2,1)}) %all-gather.2.cloned.1.call-update) | async-done | bytes 16777232 | tf_op jit(solution)/shard_map/all_gather | solution.py:26
  239.8 20.3 %fusion.13 = (f32[768]{0:T(1024)S(1)}, f32[768,4096]{1,0:T(8,128)}) fusion(bf16[2048,4096]{1,0:T(8,128)(2,1)} %all-gather.2.cloned.1.call-done, bf16[768,4096]{1,0:T(8,128)(2,1)} %constant_dynamic-update-slice_fusion, s32[]{:T(128)S(6)} %select_n.14), kind=kOutput, calls=%fused_computation.32 | convolution fusion | flops 12888046592 | bytes 32508932 | tf_op jit(solution)/shard_map/dot_general | solution.py:24
  260.1 6.1 pmax.7
  266.3 7.1 fusion
  273.4 6.1 psum.57
  279.5 11.3 %fusion.11 = (f32[4096]{0:T(1024)S(1)}, f32[768,4096]{1,0:T(8,128)}) fusion(f32[768]{0:T(1024)S(1)} %psum.57, f32[768,4096]{1,0:T(8,128)} %get-tuple-element.14, f32[768]{0:T(1024)S(1)} %pmax.7), kind=kLoop, calls=%fused_computation.31 | loop fusion | flops 12578816 | bytes 25188352 | tf_op jit(solution)/shard_map/reduce_sum | solution.py:39
  290.8 34.6 %psum.58 = f32[4096]{0:T(1024)S(1)} all-reduce(f32[4096]{0:T(1024)S(1)} %get-tuple-element.11), channel_id=1, replica_groups=mesh['rows'=8,'cls'=4] {'rows'}, use_global_device_ids=true, to_apply=%region_7.8 | all-reduce | flops 4096 | bytes 32768 | tf_op jit(solution)/shard_map/psum | solution.py:39
  325.5 5.5 multiply_reduce_fusion.2
  330.9 5.8 psum.59
  336.7 6.4 fusion.9
  343.2 33.2 %psum.60 = f32[4096]{0:T(1024)S(1)} all-reduce(f32[4096]{0:T(1024)S(1)} %fusion.9), channel_id=1, replica_groups=mesh['rows'=8,'cls'=4] {'rows'}, use_global_device_ids=true, to_apply=%region_11.12 | all-reduce | flops 4096 | bytes 32768 | tf_op jit(solution)/shard_map/psum | solution.py:39
  376.3 6.0 multiply_reduce_fusion.1
  382.3 5.8 psum.61
  388.1 11.3 %fusion.10 = (f32[4096]{0:T(1024)S(1)}, f32[768,4096]{1,0:T(8,128)}) fusion(f32[768]{0:T(1024)S(1)} %psum.61, f32[4096]{0:T(1024)S(1)} %broadcast_divide_fusion.1, f32[768]{0:T(1024)S(1)} %psum.59, f32[768,4096]{1,0:T(8,128)} %get-tuple-element.12, f32[4096]{0:T(1024)S(1)} %broadcast_divide_fusion.2), kind=kLoop, calls=%fused_computation.30 | loop fusion | flops 15724544 | bytes 25221120 | tf_op jit(solution)/shard_map/reduce_sum | solution.py:39
  399.4 33.0 %psum.62 = f32[4096]{0:T(1024)S(1)} all-reduce(f32[4096]{0:T(1024)S(1)} %get-tuple-element.9), channel_id=1, replica_groups=mesh['rows'=8,'cls'=4] {'rows'}, use_global_device_ids=true, to_apply=%region_15.16 | all-reduce | flops 4096 | bytes 32768 | tf_op jit(solution)/shard_map/psum | solution.py:39
  432.3 5.5 multiply_reduce_fusion
  437.8 5.9 all-reduce
  443.7 24.4 %convolution_convert_fusion = bf16[2048,4096]{1,0:T(8,128)(2,1)} fusion(f32[768,4096]{1,0:T(8,128)} %get-tuple-element.10, f32[768,4096]{1,0:T(8,128)} %get-tuple-element.14, f32[768]{0:T(1024)S(1)} %get-tuple-element.7, f32[4096]{0:T(1024)S(1)} %broadcast_divide_fusion, f32[768]{0:T(1024)S(1)} %get-tuple-element.8, f32[768]{0:T(1024)S(1)} %pmax.7, ...), kind=kOutput, calls=%fused_computation | convolution fusion | flops 12918456320 | bytes 45114372 | tf_op jit(solution)/shard_map/dot_general | solution.py:47
  468.1 277.9 %reduce-scatter.2.cloned.1.call-done = bf16[256,4096]{1,0:T(8,128)(2,1)} async-done(((bf16[2048,4096]{1,0:T(8,128)(2,1)}), bf16[256,4096]{1,0:T(8,128)(2,1)}) %reduce-scatter.2.cloned.1.call-update) | async-done | bytes 2097168 | tf_op jit(solution)/shard_map/reduce_scatter | solution.py:46
  746.0 4.1 convert_element_type.11
  (19 shorter events, 8.4 us)
Async XLA Ops:
  6.5 44.1 %copy-start = (bf16[768,512]{1,0:T(8,128)(2,1)S(1)}, bf16[768,512]{1,0:T(8,128)(2,1)}, u32[]{:S(2)}) copy-start(bf16[768,512]{1,0:T(8,128)(2,1)} %param.2) | copy-start | bytes 2359300
  6.5 233.3 %all-gather.2.cloned.1.call-start = ((), (), s32[]{:S(2)}) async-start(), calls=%async_computation.1 | async-start | bytes 18874368 | tf_op jit(solution)/shard_map/all_gather | solution.py:26
  7.3 738.8 %reduce-scatter.2.cloned.1.call-start = ((), (), s32[]{:S(2)}) async-start(), calls=%async_computation.2 | async-start | bytes 18874368 | tf_op jit(solution)/shard_map/reduce_scatter | solution.py:46
  7.3 12.3 %collective-permute-start = (bf16[768,512]{1,0:T(8,128)(2,1)}, bf16[768,512]{1,0:T(8,128)(2,1)S(1)}, u32[]{:S(2)}, u32[]{:S(2)}) collective-permute-start(bf16[768,512]{1,0:T(8,128)(2,1)} %param.2), channel_id=1, source_target_pairs={{0,1},{1,2},{2,3},{3,0},{4,5},{5,6},{6,7},{7,4},{8,9},{9,10},{10,1... | collective-permute-start | bytes 2359304 | tf_op jit(solution)/shard_map/ppermute | solution.py:14
  19.6 11.4 %collective-permute-start.1 = (bf16[768,512]{1,0:T(8,128)(2,1)S(1)}, bf16[768,512]{1,0:T(8,128)(2,1)S(1)}, u32[]{:S(2)}, u32[]{:S(2)}) collective-permute-start(bf16[768,512]{1,0:T(8,128)(2,1)S(1)} %collective-permute-done), channel_id=1, source_target_pairs={{0,1},{1,2},{2,3},{3,0},{4,5},{5,6},{6,7},{7,4},{8,9},{9,10},{10,1... | collective-permute-start | bytes 2359304 | tf_op jit(solution)/shard_map/ppermute | solution.py:14
  31.0 11.4 %collective-permute-start.2 = (bf16[768,512]{1,0:T(8,128)(2,1)S(1)}, bf16[768,512]{1,0:T(8,128)(2,1)S(1)}, u32[]{:S(2)}, u32[]{:S(2)}) collective-permute-start(bf16[768,512]{1,0:T(8,128)(2,1)S(1)} %collective-permute-done.1), channel_id=1, source_target_pairs={{0,1},{1,2},{2,3},{3,0},{4,5},{5,6},{6,7},{7,4},{8,9},{9,10},{10,1... | collective-permute-start | bytes 2359304 | tf_op jit(solution)/shard_map/ppermute | solution.py:14
Sparse Core Ops, SparseCore 0:
  9.5 230.3 all-gather.1
  468.2 277.7 reduce-scatter.1
